TPU v7x, 256 devices: a whole 4x4x8 slice. The times are simulated.
256 devices in a mesh: req: 32 (over y, x, core), head: 8 (over z).
Axes of the slice: x: 4, y: 4, z: 8, core: 2. Of those that a mesh axis runs over, the one named last changes fastest.
Arguments:
- queries: bfloat16 [1024, 16384], P(('req', 'head')), may hold values from -15 to 15
- cache_keys: bfloat16 [8, 32768, 1024], P(None, 'req', 'head'), may hold values from -6 to 6
- cache_values: bfloat16 [8, 32768, 1024], P(None, 'req', 'head'), may hold values from -6 to 6
- tree_keys: bfloat16 [1024, 1024], P('req', 'head'), may hold values from -10 to 10
- tree_values: bfloat16 [1024, 1024], P('req', 'head'), may hold values from -6 to 6
- parents: int32 [8, 128], replicated, may hold values from -1 to 126, as said below
- tree_sizes: int32 [8], replicated, may hold values from 16 to 128
- cache_lens: int32 [8], replicated, may hold values from 2 to 32768
Outputs:
- attended: bfloat16 [1024, 16384], P('req', 'head')
Inputs may be any that keep to these rules, and one draw needn't show every extreme that they name: parents[a, 0] = -1 (the root); for node i >= 1, parents[a, i] is a node of 0 to i - 1.
All inputs are finite; a program needn't handle non-finite values.
Results may differ from a plain program's by a relative error of at most 0.003.
Values may be sent and summed in bfloat16 or wider, within the bound.
A program may use at most 128 MiB of HBM per device.

v0:
```python
import math
import jax
import jax.numpy as jnp
from jax import lax
from jax.sharding import Mesh
from jax.sharding import PartitionSpec as P

NH = 128
KVH = 8
HD = 128
negative_fill = -1e30


def ancestry(parents):
    node_count = parents.shape[1]
    node_ids = jnp.arange(node_count, dtype=jnp.int32)
    linked = jnp.logical_or(
        parents[:, :, None] == node_ids[None, None, :], node_ids[:, None] == node_ids[None, :]
    )
    reached = linked.astype(jnp.bfloat16)
    for doubling in range((node_count - 1).bit_length()):
        squared = jnp.einsum("aij,ajk->aik", reached, reached, preferred_element_type=jnp.float32)
        reached = jnp.minimum(squared, 1.0).astype(jnp.bfloat16)
    return reached


def body(
    queries, cache_keys, cache_values, tree_keys, tree_values, parents, tree_sizes, cache_lens
):
    group_size = NH // KVH
    softmax_scale = 1.0 / math.sqrt(HD)
    request = lax.axis_index("rh")
    quarter = lax.axis_index("rl")
    n_lo = lax.axis_size("rl")
    n_hi = lax.axis_size("rh")
    cache_block = cache_keys.shape[1]
    kv_local = cache_keys.shape[2] // HD
    heads_local = kv_local * group_size
    node_count = parents.shape[1]
    rows_owned = tree_keys.shape[0]
    by_head = lax.all_to_all(queries, "head", split_axis=1, concat_axis=0, tiled=True)
    query_block = lax.all_gather(by_head, "rl", axis=0, tiled=True)
    query_block = query_block.reshape(node_count, kv_local, group_size, HD)
    both = jnp.concatenate([cache_keys, cache_values], axis=2)
    mine = lax.all_to_all(both, "rh", split_axis=0, concat_axis=1, tiled=True)[0]
    mine = mine.reshape(n_hi, cache_block, 2, kv_local, HD)
    reached = ancestry(parents)
    ancestors = lax.dynamic_index_in_dim(reached, request, 0, keepdims=False)
    ancestors = lax.dynamic_slice_in_dim(ancestors, quarter * rows_owned, rows_owned, 1)
    live_tree_all = ancestors > 0.5
    length = lax.dynamic_index_in_dim(cache_lens, request, 0, keepdims=False)
    local_tree_keys = tree_keys.reshape(rows_owned, kv_local, HD)
    local_tree_values = tree_values.reshape(rows_owned, kv_local, HD)

    def one_group(s):
        block = s * n_lo + quarter
        positions = block * cache_block + jnp.arange(cache_block, dtype=jnp.int32)
        live_cache = positions < length
        live_tree = jnp.logical_and(live_tree_all, s == request)
        block_keys = mine[s, :, 0]
        block_values = mine[s, :, 1]
        cache_scores = (
            jnp.einsum(
                "igqd,pgd->igqp", query_block, block_keys, preferred_element_type=jnp.float32
            )
            * softmax_scale
        )
        cache_scores = jnp.where(live_cache[None, None, None, :], cache_scores, negative_fill)
        tree_scores = (
            jnp.einsum(
                "igqd,rgd->igqr", query_block, local_tree_keys, preferred_element_type=jnp.float32
            )
            * softmax_scale
        )
        tree_scores = jnp.where(live_tree[:, None, None, :], tree_scores, negative_fill)
        peaks = jnp.maximum(jnp.max(cache_scores, axis=3), jnp.max(tree_scores, axis=3))
        cache_weights = jnp.where(
            live_cache[None, None, None, :], jnp.exp(cache_scores - peaks[..., None]), 0.0
        )
        tree_weights = jnp.where(
            live_tree[:, None, None, :], jnp.exp(tree_scores - peaks[..., None]), 0.0
        )
        totals = jnp.sum(cache_weights, axis=3) + jnp.sum(tree_weights, axis=3)
        group_sums = jnp.einsum(
            "igqp,pgd->igqd",
            cache_weights.astype(jnp.bfloat16),
            block_values,
            preferred_element_type=jnp.float32,
        )
        group_sums = group_sums + jnp.einsum(
            "igqr,rgd->igqd",
            tree_weights.astype(jnp.bfloat16),
            local_tree_values,
            preferred_element_type=jnp.float32,
        )
        floored = jnp.maximum(totals, 1.0)
        partial_value = group_sums / floored[..., None]
        log_total = peaks + jnp.log(floored)
        return (
            partial_value.reshape(node_count, heads_local, HD),
            log_total.reshape(node_count, heads_local),
        )

    partials, log_totals = lax.map(one_group, jnp.arange(n_hi, dtype=jnp.int32))
    top = jnp.max(log_totals, axis=0)
    weights = jnp.exp(log_totals - top)
    den = jnp.sum(weights, axis=0)
    acc = jnp.sum(weights[..., None] * partials, axis=0)
    payload = jnp.concatenate(
        [acc.reshape(node_count, heads_local * HD), den, top], axis=1
    ).reshape(n_lo, rows_owned, heads_local * HD + 2 * heads_local)
    gathered = lax.all_to_all(payload, "rl", split_axis=0, concat_axis=0, tiled=True)
    got_acc = gathered[:, :, : heads_local * HD].reshape(n_lo, rows_owned, heads_local, HD)
    got_den = gathered[:, :, heads_local * HD : heads_local * HD + heads_local]
    got_top = gathered[:, :, heads_local * HD + heads_local :]
    highest = jnp.max(got_top, axis=0)
    scale = jnp.exp(got_top - highest)
    num = jnp.sum(scale[..., None] * got_acc, axis=0)
    total = jnp.sum(scale * got_den, axis=0)
    merged = (num / total[..., None]).reshape(rows_owned, heads_local * HD)
    row_nodes = quarter * rows_owned + jnp.arange(rows_owned, dtype=jnp.int32)
    live_size = lax.dynamic_index_in_dim(tree_sizes, request, 0, keepdims=False)
    live_rows = row_nodes < live_size
    return jnp.where(live_rows[:, None], merged, 0.0).astype(jnp.bfloat16)


def solution(mesh):

    def run(
        queries, cache_keys, cache_values, tree_keys, tree_values, parents, tree_sizes, cache_lens
    ):
        n_hi = cache_keys.shape[0]
        n_lo = mesh.shape["req"] // n_hi
        split = Mesh(mesh.devices.reshape(n_hi, n_lo, mesh.shape["head"]), ("rh", "rl", "head"))
        rows = ("rh", "rl")
        placed = (
            P(("rh", "rl", "head"), None),
            P(None, rows, "head"),
            P(None, rows, "head"),
            P(rows, "head"),
            P(rows, "head"),
            P(),
            P(),
            P(),
        )
        return jax.shard_map(
            body, mesh=split, in_specs=placed, out_specs=P(rows, "head"), check_vma=False
        )(
            queries,
            cache_keys,
            cache_values,
            tree_keys,
            tree_values,
            parents,
            tree_sizes,
            cache_lens,
        )

    return run
```

profile of v0, /device:TPU:1, one launch (start us, length us, event | category | flops | bytes accessed | tf_op | source)
XLA Modules:
  0.0 273.4 jit_solution(10835699050133776124)
XLA Ops:
  0.0 9.1 %all-to-all-start.1 = ((bf16[4,8,2048]{2,0,1:T(4,128)(2,1)}), bf16[4,8,2048]{2,0,1:T(4,128)(2,1)S(1)}, u32[]{:S(2)}, u32[]{:S(2)}) async-start(bf16[4,8,2048]{2,0,1:T(4,128)(2,1)} %bitcast.168), calls=%async_computation.1 | async-start | bytes 262144 | tf_op jit(solution)/shard_map/all_to_all | solution.py:41
  9.2 2.9 %copy.62 = bf16[8,1024,128]{1,2,0:T(8,128)(2,1)S(1)} copy(bf16[8,1024,128]{2,1,0:T(8,128)(2,1)} %param.12) | data formatting | bytes 4194304 | tf_op args[2]
  12.0 3.9 %copy.61 = bf16[8,1024,128]{1,2,0:T(8,128)(2,1)} copy(bf16[8,1024,128]{2,1,0:T(8,128)(2,1)} %param.11) | data formatting | bytes 4194304 | tf_op args[1]
  16.0 4.2 %pad_maximum_fusion = bf16[8,1024,256]{1,2,0:T(8,128)(2,1)} fusion(bf16[8,1024,128]{1,2,0:T(8,128)(2,1)S(1)} %copy.62, bf16[8,1024,128]{1,2,0:T(8,128)(2,1)} %copy.61), kind=kLoop, calls=%fused_computation.47 | loop fusion | flops 8388608 | bytes 8388608 | tf_op jit(solution)/shard_map/concatenate | solution.py:44
  20.2 6.7 %all-to-all-start = ((bf16[8,1024,256]{1,2,0:T(8,128)(2,1)}), bf16[8,1024,256]{1,2,0:T(8,128)(2,1)}, u32[]{:S(2)}, u32[]{:S(2)}) async-start(bf16[8,1024,256]{1,2,0:T(8,128)(2,1)} %pad_maximum_fusion), calls=%async_computation | async-start | bytes 8388608 | tf_op jit(solution)/shard_map/all_to_all | solution.py:45
  29.7 47.9 %all_gather.3 = bf16[128,2048]{1,0:T(8,128)(2,1)S(1)} all-gather(bf16[32,2048]{1,0:T(8,128)(2,1)S(1)} %all_to_all.28), channel_id=1, replica_groups=mesh['rh'=8,'rl'=4,'head'=8] {'rl'}, dimensions={0}, use_global_device_ids=true | all-gather | bytes 655360 | tf_op jit(solution)/shard_map/all_gather | solution.py:42
  78.5 6.5 %copy.69 = bf16[8,1024,2,1,128]{4,1,3,2,0:T(8,128)(2,1)} copy(bf16[8,1024,2,1,128]{1,4,2,0,3:T(8,128)(2,1)} %bitcast.20) | data formatting | bytes 8388608 | tf_op jit(solution)/shard_map/while | solution.py:104
  85.0 160.4 %while.14 = (s32[]{:T(128)}, f32[8,128,16,128]{1,3,2,0:T(8,128)}, f32[8,128,16]{1,2,0:T(8,128)S(1)}, s32[8]{0:T(128)S(1)}, bf16[8,1024,2,1,128]{4,1,3,2,0:T(8,12...) while((s32[]{:T(128)}, f32[8,128,16,128]{1,3,2,0:T(8,128)}, ...), condition=%wide.region_5.6_spmd, body=%wide.region_0.5_spmd.sunk | while | flops 1119164416 | bytes 55485768 | solution.py:104
  88.9 5.5 %bitcast_reduce_fusion.2 = (f32[128,16]{0,1:T(8,128)S(1)}, f32[1024,128,16]{1,0,2:T(8,128)}) fusion(pred[1024]{0:T(1024)(128)(4,1)S(1)} %add_compare_fusion.3, bf16[128,1,16,128]{3,0,2,1:T(8,128)(2,1)S(1)} %get-tuple-element.349, bf16[8,1024,2,1,128]{4,1,3,2,0:T(8,128)(2,1)} %get-tuple-element.346, s32[]{:T(128)S(6)} %select_n.118), kind=kOutput, calls=%fused_computation.1.clone.1 | convolution fusion | flops 543160320 | bytes 9184260 | tf_op jit(solution)/shard_map/while/body/eval_jaxpr/igqd,pgd->igqp/dot_general | solution.py:63
  95.2 5.8 %fusion.85 = f32[128,128,16]{1,0,2:T(8,128)S(1)} fusion(f32[1024,128,16]{1,0,2:T(8,128)} %get-tuple-element.304, f32[128,16]{0,1:T(8,128)S(1)} %max.47, pred[1024]{0:T(1024)(128)(4,1)S(1)} %add_compare_fusion.3, bf16[8,1024,2,1,128]{4,1,3,2,0:T(8,128)(2,1)} %get-tuple-element.346, s32[]{:T(128)S(6)} %select_n.118), kind=kOutput, calls=%fused_computation.8.clone.1 | convolution fusion | flops 547356672 | bytes 9709572 | tf_op jit(solution)/shard_map/while/body/eval_jaxpr/igqp,pgd->igqd/dot_general | solution.py:84
  101.0 2.5 fusion.86
  108.9 5.5 %bitcast_reduce_fusion.2 = (f32[128,16]{0,1:T(8,128)S(1)}, f32[1024,128,16]{1,0,2:T(8,128)}) fusion(pred[1024]{0:T(1024)(128)(4,1)S(1)} %add_compare_fusion.3, bf16[128,1,16,128]{3,0,2,1:T(8,128)(2,1)S(1)} %get-tuple-element.349, bf16[8,1024,2,1,128]{4,1,3,2,0:T(8,128)(2,1)} %get-tuple-element.346, s32[]{:T(128)S(6)} %select_n.118), kind=kOutput, calls=%fused_computation.1.clone.1 | convolution fusion | flops 543160320 | bytes 9184260 | tf_op jit(solution)/shard_map/while/body/eval_jaxpr/igqd,pgd->igqp/dot_general | solution.py:63
  115.2 5.8 %fusion.85 = f32[128,128,16]{1,0,2:T(8,128)S(1)} fusion(f32[1024,128,16]{1,0,2:T(8,128)} %get-tuple-element.304, f32[128,16]{0,1:T(8,128)S(1)} %max.47, pred[1024]{0:T(1024)(128)(4,1)S(1)} %add_compare_fusion.3, bf16[8,1024,2,1,128]{4,1,3,2,0:T(8,128)(2,1)} %get-tuple-element.346, s32[]{:T(128)S(6)} %select_n.118), kind=kOutput, calls=%fused_computation.8.clone.1 | convolution fusion | flops 547356672 | bytes 9709572 | tf_op jit(solution)/shard_map/while/body/eval_jaxpr/igqp,pgd->igqd/dot_general | solution.py:84
  121.1 2.5 fusion.86
  129.0 5.5 %bitcast_reduce_fusion.2 = (f32[128,16]{0,1:T(8,128)S(1)}, f32[1024,128,16]{1,0,2:T(8,128)}) fusion(pred[1024]{0:T(1024)(128)(4,1)S(1)} %add_compare_fusion.3, bf16[128,1,16,128]{3,0,2,1:T(8,128)(2,1)S(1)} %get-tuple-element.349, bf16[8,1024,2,1,128]{4,1,3,2,0:T(8,128)(2,1)} %get-tuple-element.346, s32[]{:T(128)S(6)} %select_n.118), kind=kOutput, calls=%fused_computation.1.clone.1 | convolution fusion | flops 543160320 | bytes 9184260 | tf_op jit(solution)/shard_map/while/body/eval_jaxpr/igqd,pgd->igqp/dot_general | solution.py:63
  135.3 5.8 %fusion.85 = f32[128,128,16]{1,0,2:T(8,128)S(1)} fusion(f32[1024,128,16]{1,0,2:T(8,128)} %get-tuple-element.304, f32[128,16]{0,1:T(8,128)S(1)} %max.47, pred[1024]{0:T(1024)(128)(4,1)S(1)} %add_compare_fusion.3, bf16[8,1024,2,1,128]{4,1,3,2,0:T(8,128)(2,1)} %get-tuple-element.346, s32[]{:T(128)S(6)} %select_n.118), kind=kOutput, calls=%fused_computation.8.clone.1 | convolution fusion | flops 547356672 | bytes 9709572 | tf_op jit(solution)/shard_map/while/body/eval_jaxpr/igqp,pgd->igqd/dot_general | solution.py:84
  141.2 2.5 fusion.86
  149.1 5.5 %bitcast_reduce_fusion.2 = (f32[128,16]{0,1:T(8,128)S(1)}, f32[1024,128,16]{1,0,2:T(8,128)}) fusion(pred[1024]{0:T(1024)(128)(4,1)S(1)} %add_compare_fusion.3, bf16[128,1,16,128]{3,0,2,1:T(8,128)(2,1)S(1)} %get-tuple-element.349, bf16[8,1024,2,1,128]{4,1,3,2,0:T(8,128)(2,1)} %get-tuple-element.346, s32[]{:T(128)S(6)} %select_n.118), kind=kOutput, calls=%fused_computation.1.clone.1 | convolution fusion | flops 543160320 | bytes 9184260 | tf_op jit(solution)/shard_map/while/body/eval_jaxpr/igqd,pgd->igqp/dot_general | solution.py:63
  155.3 5.8 %fusion.85 = f32[128,128,16]{1,0,2:T(8,128)S(1)} fusion(f32[1024,128,16]{1,0,2:T(8,128)} %get-tuple-element.304, f32[128,16]{0,1:T(8,128)S(1)} %max.47, pred[1024]{0:T(1024)(128)(4,1)S(1)} %add_compare_fusion.3, bf16[8,1024,2,1,128]{4,1,3,2,0:T(8,128)(2,1)} %get-tuple-element.346, s32[]{:T(128)S(6)} %select_n.118), kind=kOutput, calls=%fused_computation.8.clone.1 | convolution fusion | flops 547356672 | bytes 9709572 | tf_op jit(solution)/shard_map/while/body/eval_jaxpr/igqp,pgd->igqd/dot_general | solution.py:84
  161.2 2.5 fusion.86
  169.1 5.5 %bitcast_reduce_fusion.2 = (f32[128,16]{0,1:T(8,128)S(1)}, f32[1024,128,16]{1,0,2:T(8,128)}) fusion(pred[1024]{0:T(1024)(128)(4,1)S(1)} %add_compare_fusion.3, bf16[128,1,16,128]{3,0,2,1:T(8,128)(2,1)S(1)} %get-tuple-element.349, bf16[8,1024,2,1,128]{4,1,3,2,0:T(8,128)(2,1)} %get-tuple-element.346, s32[]{:T(128)S(6)} %select_n.118), kind=kOutput, calls=%fused_computation.1.clone.1 | convolution fusion | flops 543160320 | bytes 9184260 | tf_op jit(solution)/shard_map/while/body/eval_jaxpr/igqd,pgd->igqp/dot_general | solution.py:63
  175.4 5.8 %fusion.85 = f32[128,128,16]{1,0,2:T(8,128)S(1)} fusion(f32[1024,128,16]{1,0,2:T(8,128)} %get-tuple-element.304, f32[128,16]{0,1:T(8,128)S(1)} %max.47, pred[1024]{0:T(1024)(128)(4,1)S(1)} %add_compare_fusion.3, bf16[8,1024,2,1,128]{4,1,3,2,0:T(8,128)(2,1)} %get-tuple-element.346, s32[]{:T(128)S(6)} %select_n.118), kind=kOutput, calls=%fused_computation.8.clone.1 | convolution fusion | flops 547356672 | bytes 9709572 | tf_op jit(solution)/shard_map/while/body/eval_jaxpr/igqp,pgd->igqd/dot_general | solution.py:84
  181.2 2.5 fusion.86
  189.1 5.5 %bitcast_reduce_fusion.2 = (f32[128,16]{0,1:T(8,128)S(1)}, f32[1024,128,16]{1,0,2:T(8,128)}) fusion(pred[1024]{0:T(1024)(128)(4,1)S(1)} %add_compare_fusion.3, bf16[128,1,16,128]{3,0,2,1:T(8,128)(2,1)S(1)} %get-tuple-element.349, bf16[8,1024,2,1,128]{4,1,3,2,0:T(8,128)(2,1)} %get-tuple-element.346, s32[]{:T(128)S(6)} %select_n.118), kind=kOutput, calls=%fused_computation.1.clone.1 | convolution fusion | flops 543160320 | bytes 9184260 | tf_op jit(solution)/shard_map/while/body/eval_jaxpr/igqd,pgd->igqp/dot_general | solution.py:63
  195.4 5.8 %fusion.85 = f32[128,128,16]{1,0,2:T(8,128)S(1)} fusion(f32[1024,128,16]{1,0,2:T(8,128)} %get-tuple-element.304, f32[128,16]{0,1:T(8,128)S(1)} %max.47, pred[1024]{0:T(1024)(128)(4,1)S(1)} %add_compare_fusion.3, bf16[8,1024,2,1,128]{4,1,3,2,0:T(8,128)(2,1)} %get-tuple-element.346, s32[]{:T(128)S(6)} %select_n.118), kind=kOutput, calls=%fused_computation.8.clone.1 | convolution fusion | flops 547356672 | bytes 9709572 | tf_op jit(solution)/shard_map/while/body/eval_jaxpr/igqp,pgd->igqd/dot_general | solution.py:84
  209.2 5.5 %bitcast_reduce_fusion.2 = (f32[128,16]{0,1:T(8,128)S(1)}, f32[1024,128,16]{1,0,2:T(8,128)}) fusion(pred[1024]{0:T(1024)(128)(4,1)S(1)} %add_compare_fusion.3, bf16[128,1,16,128]{3,0,2,1:T(8,128)(2,1)S(1)} %get-tuple-element.349, bf16[8,1024,2,1,128]{4,1,3,2,0:T(8,128)(2,1)} %get-tuple-element.346, s32[]{:T(128)S(6)} %select_n.118), kind=kOutput, calls=%fused_computation.1.clone.1 | convolution fusion | flops 543160320 | bytes 9184260 | tf_op jit(solution)/shard_map/while/body/eval_jaxpr/igqd,pgd->igqp/dot_general | solution.py:63
  215.5 5.8 %fusion.85 = f32[128,128,16]{1,0,2:T(8,128)S(1)} fusion(f32[1024,128,16]{1,0,2:T(8,128)} %get-tuple-element.304, f32[128,16]{0,1:T(8,128)S(1)} %max.47, pred[1024]{0:T(1024)(128)(4,1)S(1)} %add_compare_fusion.3, bf16[8,1024,2,1,128]{4,1,3,2,0:T(8,128)(2,1)} %get-tuple-element.346, s32[]{:T(128)S(6)} %select_n.118), kind=kOutput, calls=%fused_computation.8.clone.1 | convolution fusion | flops 547356672 | bytes 9709572 | tf_op jit(solution)/shard_map/while/body/eval_jaxpr/igqp,pgd->igqd/dot_general | solution.py:84
  229.3 5.5 %bitcast_reduce_fusion.2 = (f32[128,16]{0,1:T(8,128)S(1)}, f32[1024,128,16]{1,0,2:T(8,128)}) fusion(pred[1024]{0:T(1024)(128)(4,1)S(1)} %add_compare_fusion.3, bf16[128,1,16,128]{3,0,2,1:T(8,128)(2,1)S(1)} %get-tuple-element.349, bf16[8,1024,2,1,128]{4,1,3,2,0:T(8,128)(2,1)} %get-tuple-element.346, s32[]{:T(128)S(6)} %select_n.118), kind=kOutput, calls=%fused_computation.1.clone.1 | convolution fusion | flops 543160320 | bytes 9184260 | tf_op jit(solution)/shard_map/while/body/eval_jaxpr/igqd,pgd->igqp/dot_general | solution.py:63
  235.5 5.8 %fusion.85 = f32[128,128,16]{1,0,2:T(8,128)S(1)} fusion(f32[1024,128,16]{1,0,2:T(8,128)} %get-tuple-element.304, f32[128,16]{0,1:T(8,128)S(1)} %max.47, pred[1024]{0:T(1024)(128)(4,1)S(1)} %add_compare_fusion.3, bf16[8,1024,2,1,128]{4,1,3,2,0:T(8,128)(2,1)} %get-tuple-element.346, s32[]{:T(128)S(6)} %select_n.118), kind=kOutput, calls=%fused_computation.8.clone.1 | convolution fusion | flops 547356672 | bytes 9709572 | tf_op jit(solution)/shard_map/while/body/eval_jaxpr/igqp,pgd->igqd/dot_general | solution.py:84
  245.5 4.8 %multiply_reduce_fusion = f32[128,16,128]{0,2,1:T(8,128)S(1)} fusion(f32[8,128,16,128]{1,3,2,0:T(8,128)} %get-tuple-element.146, f32[8,128,16]{1,2,0:T(8,128)S(1)} %get-tuple-element.224), kind=kLoop, calls=%fused_computation.46 | loop fusion | flops 3932160 | bytes 9502720 | tf_op jit(solution)/shard_map/reduce_sum | solution.py:108
  252.2 5.2 %all-to-all-start.2 = ((f32[4,32,2080]{2,1,0:T(8,128)}), f32[4,32,2080]{2,1,0:T(8,128)S(1)}, u32[]{:S(2)}, u32[]{:S(2)}) async-start(f32[4,32,2080]{2,1,0:T(8,128)} %concatenate.17), calls=%async_computation.2 | async-start | bytes 2228224 | tf_op jit(solution)/shard_map/all_to_all | solution.py:112
  258.7 13.1 %all-to-all-done.2 = f32[4,32,2080]{2,1,0:T(8,128)S(1)} async-done(((f32[4,32,2080]{2,1,0:T(8,128)}), f32[4,32,2080]{2,1,0:T(8,128)S(1)}, u32[]{:S(2)}, u32[]{:S(2)}) %all-to-all-start.2) | async-done | bytes 1064992 | tf_op jit(solution)/shard_map/all_to_all | solution.py:112
  (150 shorter events, 38.4 us)
Async XLA Ops:
  0.0 78.3 %copy-start = (bf16[32,128]{1,0:T(8,128)(2,1)S(1)}, bf16[32,128]{1,0:T(8,128)(2,1)}, u32[]{:S(2)}) copy-start(bf16[32,128]{1,0:T(8,128)(2,1)} %param.13) | copy-start | bytes 24580
  0.0 20.2 %all-to-all-start.1 = ((bf16[4,8,2048]{2,0,1:T(4,128)(2,1)}), bf16[4,8,2048]{2,0,1:T(4,128)(2,1)S(1)}, u32[]{:S(2)}, u32[]{:S(2)}) async-start(bf16[4,8,2048]{2,0,1:T(4,128)(2,1)} %bitcast.168), calls=%async_computation.1 | async-start | bytes 262144 | tf_op jit(solution)/shard_map/all_to_all | solution.py:41
  16.0 10.9 %copy-start.3 = (s32[8]{0:T(128)S(1)}, s32[8]{0:T(128)}, u32[]{:S(2)}) copy-start(s32[8]{0:T(128)} %param.17) | copy-start | bytes 100
  16.0 11.5 %copy-start.2 = (s32[8,128]{1,0:T(8,128)S(1)}, s32[8,128]{1,0:T(8,128)}, u32[]{:S(2)}) copy-start(s32[8,128]{1,0:T(8,128)} %param.15) | copy-start | bytes 12292
  20.2 58.3 %all-to-all-start = ((bf16[8,1024,256]{1,2,0:T(8,128)(2,1)}), bf16[8,1024,256]{1,2,0:T(8,128)(2,1)}, u32[]{:S(2)}, u32[]{:S(2)}) async-start(bf16[8,1024,256]{1,2,0:T(8,128)(2,1)} %pad_maximum_fusion), calls=%async_computation | async-start | bytes 8388608 | tf_op jit(solution)/shard_map/all_to_all | solution.py:45
  26.8 58.1 %copy-start.1 = (bf16[32,128]{1,0:T(8,128)(2,1)S(1)}, bf16[32,128]{1,0:T(8,128)(2,1)}, u32[]{:S(2)}) copy-start(bf16[32,128]{1,0:T(8,128)(2,1)} %param.14) | copy-start | bytes 24580
  95.1 5.9 %slice-start = ((s8[8388608]{0:T(1024)(128)(4,1)}), s8[4194304]{0:T(1024)(128)(4,1)S(1)}, s32[]{:S(2)}) async-start(s8[8388608]{0:T(1024)(128)(4,1)} %bitcast.160), calls=%async_computation.3 | async-start | bytes 8388608 | tf_op jit(solution)/shard_map/while
  95.2 5.9 %slice-start.1 = ((s8[8388608]{0:T(1024)(128)(4,1)}), s8[4194304]{0:T(1024)(128)(4,1)S(1)}, s32[]{:S(2)}) async-start(s8[8388608]{0:T(1024)(128)(4,1)} %bitcast.160), calls=%async_computation.4 | async-start | bytes 8388608 | tf_op jit(solution)/shard_map/while
  115.1 5.9 %slice-start = ((s8[8388608]{0:T(1024)(128)(4,1)}), s8[4194304]{0:T(1024)(128)(4,1)S(1)}, s32[]{:S(2)}) async-start(s8[8388608]{0:T(1024)(128)(4,1)} %bitcast.160), calls=%async_computation.3 | async-start | bytes 8388608 | tf_op jit(solution)/shard_map/while
  115.2 5.9 %slice-start.1 = ((s8[8388608]{0:T(1024)(128)(4,1)}), s8[4194304]{0:T(1024)(128)(4,1)S(1)}, s32[]{:S(2)}) async-start(s8[8388608]{0:T(1024)(128)(4,1)} %bitcast.160), calls=%async_computation.4 | async-start | bytes 8388608 | tf_op jit(solution)/shard_map/while
  135.2 5.9 %slice-start = ((s8[8388608]{0:T(1024)(128)(4,1)}), s8[4194304]{0:T(1024)(128)(4,1)S(1)}, s32[]{:S(2)}) async-start(s8[8388608]{0:T(1024)(128)(4,1)} %bitcast.160), calls=%async_computation.3 | async-start | bytes 8388608 | tf_op jit(solution)/shard_map/while
  135.3 5.9 %slice-start.1 = ((s8[8388608]{0:T(1024)(128)(4,1)}), s8[4194304]{0:T(1024)(128)(4,1)S(1)}, s32[]{:S(2)}) async-start(s8[8388608]{0:T(1024)(128)(4,1)} %bitcast.160), calls=%async_computation.4 | async-start | bytes 8388608 | tf_op jit(solution)/shard_map/while
  155.2 5.9 %slice-start = ((s8[8388608]{0:T(1024)(128)(4,1)}), s8[4194304]{0:T(1024)(128)(4,1)S(1)}, s32[]{:S(2)}) async-start(s8[8388608]{0:T(1024)(128)(4,1)} %bitcast.160), calls=%async_computation.3 | async-start | bytes 8388608 | tf_op jit(solution)/shard_map/while
  155.3 5.9 %slice-start.1 = ((s8[8388608]{0:T(1024)(128)(4,1)}), s8[4194304]{0:T(1024)(128)(4,1)S(1)}, s32[]{:S(2)}) async-start(s8[8388608]{0:T(1024)(128)(4,1)} %bitcast.160), calls=%async_computation.4 | async-start | bytes 8388608 | tf_op jit(solution)/shard_map/while
  175.3 5.9 %slice-start = ((s8[8388608]{0:T(1024)(128)(4,1)}), s8[4194304]{0:T(1024)(128)(4,1)S(1)}, s32[]{:S(2)}) async-start(s8[8388608]{0:T(1024)(128)(4,1)} %bitcast.160), calls=%async_computation.3 | async-start | bytes 8388608 | tf_op jit(solution)/shard_map/while
  175.4 5.9 %slice-start.1 = ((s8[8388608]{0:T(1024)(128)(4,1)}), s8[4194304]{0:T(1024)(128)(4,1)S(1)}, s32[]{:S(2)}) async-start(s8[8388608]{0:T(1024)(128)(4,1)} %bitcast.160), calls=%async_computation.4 | async-start | bytes 8388608 | tf_op jit(solution)/shard_map/while
  195.3 5.9 %slice-start = ((s8[8388608]{0:T(1024)(128)(4,1)}), s8[4194304]{0:T(1024)(128)(4,1)S(1)}, s32[]{:S(2)}) async-start(s8[8388608]{0:T(1024)(128)(4,1)} %bitcast.160), calls=%async_computation.3 | async-start | bytes 8388608 | tf_op jit(solution)/shard_map/while
  195.4 5.9 %slice-start.1 = ((s8[8388608]{0:T(1024)(128)(4,1)}), s8[4194304]{0:T(1024)(128)(4,1)S(1)}, s32[]{:S(2)}) async-start(s8[8388608]{0:T(1024)(128)(4,1)} %bitcast.160), calls=%async_computation.4 | async-start | bytes 8388608 | tf_op jit(solution)/shard_map/while
  215.4 5.9 %slice-start = ((s8[8388608]{0:T(1024)(128)(4,1)}), s8[4194304]{0:T(1024)(128)(4,1)S(1)}, s32[]{:S(2)}) async-start(s8[8388608]{0:T(1024)(128)(4,1)} %bitcast.160), calls=%async_computation.3 | async-start | bytes 8388608 | tf_op jit(solution)/shard_map/while
  215.5 5.9 %slice-start.1 = ((s8[8388608]{0:T(1024)(128)(4,1)}), s8[4194304]{0:T(1024)(128)(4,1)S(1)}, s32[]{:S(2)}) async-start(s8[8388608]{0:T(1024)(128)(4,1)} %bitcast.160), calls=%async_computation.4 | async-start | bytes 8388608 | tf_op jit(solution)/shard_map/while
  235.4 5.9 %slice-start = ((s8[8388608]{0:T(1024)(128)(4,1)}), s8[4194304]{0:T(1024)(128)(4,1)S(1)}, s32[]{:S(2)}) async-start(s8[8388608]{0:T(1024)(128)(4,1)} %bitcast.160), calls=%async_computation.3 | async-start | bytes 8388608 | tf_op jit(solution)/shard_map/while
  235.5 5.9 %slice-start.1 = ((s8[8388608]{0:T(1024)(128)(4,1)}), s8[4194304]{0:T(1024)(128)(4,1)S(1)}, s32[]{:S(2)}) async-start(s8[8388608]{0:T(1024)(128)(4,1)} %bitcast.160), calls=%async_computation.4 | async-start | bytes 8388608 | tf_op jit(solution)/shard_map/while
  245.5 11.9 %copy-start.4 = (s32[8]{0:T(128)S(1)}, s32[8]{0:T(128)}, u32[]{:S(2)}) copy-start(s32[8]{0:T(128)} %param.16) | copy-start | bytes 100
  252.2 19.5 %all-to-all-start.2 = ((f32[4,32,2080]{2,1,0:T(8,128)}), f32[4,32,2080]{2,1,0:T(8,128)S(1)}, u32[]{:S(2)}, u32[]{:S(2)}) async-start(f32[4,32,2080]{2,1,0:T(8,128)} %concatenate.17), calls=%async_computation.2 | async-start | bytes 2228224 | tf_op jit(solution)/shard_map/all_to_all | solution.py:112
where the time goes:
time: 275 us; the launch traced here: 273 us
  matrix products  103 us (37%)
  blocking collectives  47.9 us (17%)
  other arithmetic  36.8 us (13%)
  loops' own time  27.8 us (10%)
  local copies, waits for them, and re-layouts  23.5 us (9%)
  starting transfers between devices  21 us (8%)
  waiting for transfers between devices  13.1 us (5%)
    all_gather x1, blocking collectives, body(): query_block = lax.all_gather(by_head, 'rl', axis=0, tiled=True)  47.9 us
    dot_general x8, matrix products, one_group(): jnp.einsum('igqp,pgd->igqd', cache_weights.astype(jnp.bfloat16), block_va...  46.3 us
    dot_general x8, matrix products, one_group(): jnp.einsum('igqd,pgd->igqp', query_block, block_keys, preferred_element_t...  43.9 us
    another operation x1, loops' own time, body(): partials, log_totals = lax.map(one_group, jnp.arange(n_hi, dtype=jnp.int32))  27.8 us
    reduce_sum x16, other arithmetic, one_group(): totals = jnp.sum(cache_weights, axis=3) + jnp.sum(tree_weights, axis=3)  20.8 us
    all_to_all x1, waiting for transfers between devices, body(): lax.all_to_all(payload, 'rl', split_axis=0, concat_axis=0, tiled=True)  13.1 us
    dot_general x8, matrix products, one_group(): jnp.einsum('igqr,rgd->igqd', tree_weights.astype(jnp.bfloat16), local_tre...  10.8 us
    all_to_all x1, starting transfers between devices, body(): lax.all_to_all(queries, 'head', split_axis=1, concat_axis=0, tiled=True)  9.15 us
  transfers between devices with their start and end apart: 3, of which 1 were waited for; matrix products, arithmetic and copies ran while one was open for 6% of the time, Pallas kernels for 0%

commit v1 on v0

--- a/solution.py
+++ b/solution.py
@@ -39,7 +39,9 @@
     node_count = parents.shape[1]
     rows_owned = tree_keys.shape[0]
     by_head = lax.all_to_all(queries, "head", split_axis=1, concat_axis=0, tiled=True)
-    query_block = lax.all_gather(by_head, "rl", axis=0, tiled=True)
+    query_block = jnp.concatenate(
+        lax.all_to_all(jnp.stack(lax.axis_size("rl") * [by_head], axis=0), "rl", 0, 0), 0
+    )
     query_block = query_block.reshape(node_count, kv_local, group_size, HD)
     both = jnp.concatenate([cache_keys, cache_values], axis=2)
     mine = lax.all_to_all(both, "rh", split_axis=0, concat_axis=1, tiled=True)[0]

time: 275 us -> 288 us (1.047)
  waiting for transfers between devices: 13.1 us -> 60.4 us
  blocking collectives: 47.9 us -> 16.9 us
  starting transfers between devices: 21 us -> 17 us
    all_gather x1 -> x0, blocking collectives: 47.9 us -> none  [body(): query_block = lax.all_gather(by_head, 'rl', axis=0, tiled=True)]
    all_to_all x1, waiting for transfers between devices: 0.01 us -> 47.4 us  [body(): lax.all_to_all(both, 'rh', split_axis=0, concat_axis=1, tiled=True)[0]]
    all_to_all x0 -> x1, blocking collectives: none -> 16.9 us  [body(): lax.all_to_all(queries, 'head', split_axis=1, concat_axis=0, tiled=True)]
    all_to_all x1, starting transfers between devices: 9.15 us -> 5.72 us  [body(): lax.all_to_all(jnp.stack(lax.axis_size('rl') * [by_head], axis=0), 'rl',...]
    unnamed x12 -> x13, local copies, waits for them, and re-layouts: 6.81 us -> 6.93 us
  transfers between devices with their start and end apart: 3 -> 3, of which waited for: 1 -> 2; matrix products, arithmetic and copies ran while one was open for 6% -> 5% of each run, Pallas kernels for 0% -> 0%
where the time goes in v1:
time: 288 us; the launch traced here: 286 us
  matrix products  103 us (36%)
  waiting for transfers between devices  60.4 us (21%)
  other arithmetic  36.8 us (13%)
  loops' own time  27.8 us (10%)
  local copies, waits for them, and re-layouts  24 us (8%)
  starting transfers between devices  17 us (6%)
  blocking collectives  16.9 us (6%)
    all_to_all x1, waiting for transfers between devices, body(): lax.all_to_all(both, 'rh', split_axis=0, concat_axis=1, tiled=True)[0]  47.4 us
    dot_general x8, matrix products, one_group(): jnp.einsum('igqp,pgd->igqd', cache_weights.astype(jnp.bfloat16), block_va...  46.3 us
    dot_general x8, matrix products, one_group(): jnp.einsum('igqd,pgd->igqp', query_block, block_keys, preferred_element_t...  43.9 us
    another operation x1, loops' own time, body(): partials, log_totals = lax.map(one_group, jnp.arange(n_hi, dtype=jnp.int32))  27.8 us
    reduce_sum x16, other arithmetic, one_group(): totals = jnp.sum(cache_weights, axis=3) + jnp.sum(tree_weights, axis=3)  20.8 us
    all_to_all x1, blocking collectives, body(): lax.all_to_all(queries, 'head', split_axis=1, concat_axis=0, tiled=True)  16.9 us
    all_to_all x1, waiting for transfers between devices, body(): lax.all_to_all(payload, 'rl', split_axis=0, concat_axis=0, tiled=True)  13.1 us
    dot_general x8, matrix products, one_group(): jnp.einsum('igqr,rgd->igqd', tree_weights.astype(jnp.bfloat16), local_tre...  10.8 us
  transfers between devices with their start and end apart: 3, of which 2 were waited for; matrix products, arithmetic and copies ran while one was open for 5% of the time, Pallas kernels for 0%

profile of v1, /device:TPU:1, one launch (start us, length us, event | category | flops | bytes accessed | tf_op | source)
XLA Modules:
  0.0 286.4 jit_solution(724290896041709014)
XLA Ops:
  0.0 16.9 %all_to_all.35 = bf16[4,8,2048]{2,0,1:T(4,128)(2,1)S(1)} all-to-all(bf16[4,8,2048]{2,0,1:T(4,128)(2,1)} %bitcast.174), channel_id=1, replica_groups=mesh['rh'=8,'rl'=4,'head'=8] {'head'}, dimensions={1} | all-to-all | bytes 262144 | tf_op jit(solution)/shard_map/all_to_all | solution.py:41
  17.8 5.7 %all-to-all-start.2 = ((bf16[4,32,2048]{2,1,0:T(8,128)(2,1)}), bf16[4,32,2048]{2,1,0:T(8,128)(2,1)S(1)}, u32[]{:S(2)}, u32[]{:S(2)}) async-start(bf16[4,32,2048]{2,1,0:T(8,128)(2,1)} %stack.10), calls=%async_computation.2 | async-start | bytes 1048576 | tf_op jit(solution)/shard_map/all_to_all | solution.py:43
  23.5 2.9 copy.56
  26.4 3.9 %copy.55 = bf16[8,1024,128]{1,2,0:T(8,128)(2,1)} copy(bf16[8,1024,128]{2,1,0:T(8,128)(2,1)} %param.11) | data formatting | bytes 4194304 | tf_op args[1]
  30.3 4.2 %pad_maximum_fusion = bf16[8,1024,256]{1,2,0:T(8,128)(2,1)} fusion(bf16[8,1024,128]{1,2,0:T(8,128)(2,1)S(1)} %copy.56, bf16[8,1024,128]{1,2,0:T(8,128)(2,1)} %copy.55), kind=kLoop, calls=%fused_computation.47 | loop fusion | flops 8388608 | bytes 8388608 | tf_op jit(solution)/shard_map/concatenate | solution.py:46
  34.6 6.7 %all-to-all-start = ((bf16[8,1024,256]{1,2,0:T(8,128)(2,1)}), bf16[8,1024,256]{1,2,0:T(8,128)(2,1)}, u32[]{:S(2)}, u32[]{:S(2)}) async-start(bf16[8,1024,256]{1,2,0:T(8,128)(2,1)} %pad_maximum_fusion), calls=%async_computation | async-start | bytes 8388608 | tf_op jit(solution)/shard_map/all_to_all | solution.py:47
  44.6 47.4 %all-to-all-done = bf16[8,1024,256]{1,2,0:T(8,128)(2,1)} async-done(((bf16[8,1024,256]{1,2,0:T(8,128)(2,1)}), bf16[8,1024,256]{1,2,0:T(8,128)(2,1)}, u32[]{:S(2)}, u32[]{:S(2)}) %all-to-all-start) | async-done | bytes 4194336 | tf_op jit(solution)/shard_map/all_to_all | solution.py:47
  92.0 6.4 %copy.61 = bf16[8,1024,2,1,128]{4,1,3,2,0:T(8,128)(2,1)} copy(bf16[8,1024,2,1,128]{1,4,2,0,3:T(8,128)(2,1)} %bitcast.20) | data formatting | bytes 8388608 | tf_op jit(solution)/shard_map/while | solution.py:106
  98.5 160.4 %while.14 = (s32[]{:T(128)}, f32[8,128,16,128]{1,3,2,0:T(8,128)}, f32[8,128,16]{1,2,0:T(8,128)S(1)}, s32[8]{0:T(128)S(1)}, bf16[8,1024,2,1,128]{4,1,3,2,0:T(8,12...) while((s32[]{:T(128)}, f32[8,128,16,128]{1,3,2,0:T(8,128)}, ...), condition=%wide.region_5.6_spmd, body=%wide.region_0.5_spmd.sunk | while | flops 1119164416 | bytes 55485768 | solution.py:106
  102.4 5.5 %bitcast_reduce_fusion.2 = (f32[128,16]{0,1:T(8,128)S(1)}, f32[1024,128,16]{1,0,2:T(8,128)}) fusion(pred[1024]{0:T(1024)(128)(4,1)S(1)} %add_compare_fusion.3, bf16[128,1,16,128]{3,0,2,1:T(8,128)(2,1)S(1)} %get-tuple-element.349, bf16[8,1024,2,1,128]{4,1,3,2,0:T(8,128)(2,1)} %get-tuple-element.346, s32[]{:T(128)S(6)} %select_n.118), kind=kOutput, calls=%fused_computation.1.clone.1 | convolution fusion | flops 543160320 | bytes 9184260 | tf_op jit(solution)/shard_map/while/body/eval_jaxpr/igqd,pgd->igqp/dot_general | solution.py:65
  108.7 5.8 %fusion.85 = f32[128,128,16]{1,0,2:T(8,128)S(1)} fusion(f32[1024,128,16]{1,0,2:T(8,128)} %get-tuple-element.304, f32[128,16]{0,1:T(8,128)S(1)} %max.47, pred[1024]{0:T(1024)(128)(4,1)S(1)} %add_compare_fusion.3, bf16[8,1024,2,1,128]{4,1,3,2,0:T(8,128)(2,1)} %get-tuple-element.346, s32[]{:T(128)S(6)} %select_n.118), kind=kOutput, calls=%fused_computation.8.clone.1 | convolution fusion | flops 547356672 | bytes 9709572 | tf_op jit(solution)/shard_map/while/body/eval_jaxpr/igqp,pgd->igqd/dot_general | solution.py:86
  114.5 2.5 fusion.86
  122.4 5.5 %bitcast_reduce_fusion.2 = (f32[128,16]{0,1:T(8,128)S(1)}, f32[1024,128,16]{1,0,2:T(8,128)}) fusion(pred[1024]{0:T(1024)(128)(4,1)S(1)} %add_compare_fusion.3, bf16[128,1,16,128]{3,0,2,1:T(8,128)(2,1)S(1)} %get-tuple-element.349, bf16[8,1024,2,1,128]{4,1,3,2,0:T(8,128)(2,1)} %get-tuple-element.346, s32[]{:T(128)S(6)} %select_n.118), kind=kOutput, calls=%fused_computation.1.clone.1 | convolution fusion | flops 543160320 | bytes 9184260 | tf_op jit(solution)/shard_map/while/body/eval_jaxpr/igqd,pgd->igqp/dot_general | solution.py:65
  128.7 5.8 %fusion.85 = f32[128,128,16]{1,0,2:T(8,128)S(1)} fusion(f32[1024,128,16]{1,0,2:T(8,128)} %get-tuple-element.304, f32[128,16]{0,1:T(8,128)S(1)} %max.47, pred[1024]{0:T(1024)(128)(4,1)S(1)} %add_compare_fusion.3, bf16[8,1024,2,1,128]{4,1,3,2,0:T(8,128)(2,1)} %get-tuple-element.346, s32[]{:T(128)S(6)} %select_n.118), kind=kOutput, calls=%fused_computation.8.clone.1 | convolution fusion | flops 547356672 | bytes 9709572 | tf_op jit(solution)/shard_map/while/body/eval_jaxpr/igqp,pgd->igqd/dot_general | solution.py:86
  134.6 2.5 fusion.86
  142.5 5.5 %bitcast_reduce_fusion.2 = (f32[128,16]{0,1:T(8,128)S(1)}, f32[1024,128,16]{1,0,2:T(8,128)}) fusion(pred[1024]{0:T(1024)(128)(4,1)S(1)} %add_compare_fusion.3, bf16[128,1,16,128]{3,0,2,1:T(8,128)(2,1)S(1)} %get-tuple-element.349, bf16[8,1024,2,1,128]{4,1,3,2,0:T(8,128)(2,1)} %get-tuple-element.346, s32[]{:T(128)S(6)} %select_n.118), kind=kOutput, calls=%fused_computation.1.clone.1 | convolution fusion | flops 543160320 | bytes 9184260 | tf_op jit(solution)/shard_map/while/body/eval_jaxpr/igqd,pgd->igqp/dot_general | solution.py:65
  148.8 5.8 %fusion.85 = f32[128,128,16]{1,0,2:T(8,128)S(1)} fusion(f32[1024,128,16]{1,0,2:T(8,128)} %get-tuple-element.304, f32[128,16]{0,1:T(8,128)S(1)} %max.47, pred[1024]{0:T(1024)(128)(4,1)S(1)} %add_compare_fusion.3, bf16[8,1024,2,1,128]{4,1,3,2,0:T(8,128)(2,1)} %get-tuple-element.346, s32[]{:T(128)S(6)} %select_n.118), kind=kOutput, calls=%fused_computation.8.clone.1 | convolution fusion | flops 547356672 | bytes 9709572 | tf_op jit(solution)/shard_map/while/body/eval_jaxpr/igqp,pgd->igqd/dot_general | solution.py:86
  154.7 2.5 fusion.86
  162.6 5.5 %bitcast_reduce_fusion.2 = (f32[128,16]{0,1:T(8,128)S(1)}, f32[1024,128,16]{1,0,2:T(8,128)}) fusion(pred[1024]{0:T(1024)(128)(4,1)S(1)} %add_compare_fusion.3, bf16[128,1,16,128]{3,0,2,1:T(8,128)(2,1)S(1)} %get-tuple-element.349, bf16[8,1024,2,1,128]{4,1,3,2,0:T(8,128)(2,1)} %get-tuple-element.346, s32[]{:T(128)S(6)} %select_n.118), kind=kOutput, calls=%fused_computation.1.clone.1 | convolution fusion | flops 543160320 | bytes 9184260 | tf_op jit(solution)/shard_map/while/body/eval_jaxpr/igqd,pgd->igqp/dot_general | solution.py:65
  168.8 5.8 %fusion.85 = f32[128,128,16]{1,0,2:T(8,128)S(1)} fusion(f32[1024,128,16]{1,0,2:T(8,128)} %get-tuple-element.304, f32[128,16]{0,1:T(8,128)S(1)} %max.47, pred[1024]{0:T(1024)(128)(4,1)S(1)} %add_compare_fusion.3, bf16[8,1024,2,1,128]{4,1,3,2,0:T(8,128)(2,1)} %get-tuple-element.346, s32[]{:T(128)S(6)} %select_n.118), kind=kOutput, calls=%fused_computation.8.clone.1 | convolution fusion | flops 547356672 | bytes 9709572 | tf_op jit(solution)/shard_map/while/body/eval_jaxpr/igqp,pgd->igqd/dot_general | solution.py:86
  174.7 2.5 fusion.86
  182.6 5.5 %bitcast_reduce_fusion.2 = (f32[128,16]{0,1:T(8,128)S(1)}, f32[1024,128,16]{1,0,2:T(8,128)}) fusion(pred[1024]{0:T(1024)(128)(4,1)S(1)} %add_compare_fusion.3, bf16[128,1,16,128]{3,0,2,1:T(8,128)(2,1)S(1)} %get-tuple-element.349, bf16[8,1024,2,1,128]{4,1,3,2,0:T(8,128)(2,1)} %get-tuple-element.346, s32[]{:T(128)S(6)} %select_n.118), kind=kOutput, calls=%fused_computation.1.clone.1 | convolution fusion | flops 543160320 | bytes 9184260 | tf_op jit(solution)/shard_map/while/body/eval_jaxpr/igqd,pgd->igqp/dot_general | solution.py:65
  188.9 5.8 %fusion.85 = f32[128,128,16]{1,0,2:T(8,128)S(1)} fusion(f32[1024,128,16]{1,0,2:T(8,128)} %get-tuple-element.304, f32[128,16]{0,1:T(8,128)S(1)} %max.47, pred[1024]{0:T(1024)(128)(4,1)S(1)} %add_compare_fusion.3, bf16[8,1024,2,1,128]{4,1,3,2,0:T(8,128)(2,1)} %get-tuple-element.346, s32[]{:T(128)S(6)} %select_n.118), kind=kOutput, calls=%fused_computation.8.clone.1 | convolution fusion | flops 547356672 | bytes 9709572 | tf_op jit(solution)/shard_map/while/body/eval_jaxpr/igqp,pgd->igqd/dot_general | solution.py:86
  202.6 5.5 %bitcast_reduce_fusion.2 = (f32[128,16]{0,1:T(8,128)S(1)}, f32[1024,128,16]{1,0,2:T(8,128)}) fusion(pred[1024]{0:T(1024)(128)(4,1)S(1)} %add_compare_fusion.3, bf16[128,1,16,128]{3,0,2,1:T(8,128)(2,1)S(1)} %get-tuple-element.349, bf16[8,1024,2,1,128]{4,1,3,2,0:T(8,128)(2,1)} %get-tuple-element.346, s32[]{:T(128)S(6)} %select_n.118), kind=kOutput, calls=%fused_computation.1.clone.1 | convolution fusion | flops 543160320 | bytes 9184260 | tf_op jit(solution)/shard_map/while/body/eval_jaxpr/igqd,pgd->igqp/dot_general | solution.py:65
  208.9 5.8 %fusion.85 = f32[128,128,16]{1,0,2:T(8,128)S(1)} fusion(f32[1024,128,16]{1,0,2:T(8,128)} %get-tuple-element.304, f32[128,16]{0,1:T(8,128)S(1)} %max.47, pred[1024]{0:T(1024)(128)(4,1)S(1)} %add_compare_fusion.3, bf16[8,1024,2,1,128]{4,1,3,2,0:T(8,128)(2,1)} %get-tuple-element.346, s32[]{:T(128)S(6)} %select_n.118), kind=kOutput, calls=%fused_computation.8.clone.1 | convolution fusion | flops 547356672 | bytes 9709572 | tf_op jit(solution)/shard_map/while/body/eval_jaxpr/igqp,pgd->igqd/dot_general | solution.py:86
  222.7 5.5 %bitcast_reduce_fusion.2 = (f32[128,16]{0,1:T(8,128)S(1)}, f32[1024,128,16]{1,0,2:T(8,128)}) fusion(pred[1024]{0:T(1024)(128)(4,1)S(1)} %add_compare_fusion.3, bf16[128,1,16,128]{3,0,2,1:T(8,128)(2,1)S(1)} %get-tuple-element.349, bf16[8,1024,2,1,128]{4,1,3,2,0:T(8,128)(2,1)} %get-tuple-element.346, s32[]{:T(128)S(6)} %select_n.118), kind=kOutput, calls=%fused_computation.1.clone.1 | convolution fusion | flops 543160320 | bytes 9184260 | tf_op jit(solution)/shard_map/while/body/eval_jaxpr/igqd,pgd->igqp/dot_general | solution.py:65
  229.0 5.8 %fusion.85 = f32[128,128,16]{1,0,2:T(8,128)S(1)} fusion(f32[1024,128,16]{1,0,2:T(8,128)} %get-tuple-element.304, f32[128,16]{0,1:T(8,128)S(1)} %max.47, pred[1024]{0:T(1024)(128)(4,1)S(1)} %add_compare_fusion.3, bf16[8,1024,2,1,128]{4,1,3,2,0:T(8,128)(2,1)} %get-tuple-element.346, s32[]{:T(128)S(6)} %select_n.118), kind=kOutput, calls=%fused_computation.8.clone.1 | convolution fusion | flops 547356672 | bytes 9709572 | tf_op jit(solution)/shard_map/while/body/eval_jaxpr/igqp,pgd->igqd/dot_general | solution.py:86
  242.8 5.5 %bitcast_reduce_fusion.2 = (f32[128,16]{0,1:T(8,128)S(1)}, f32[1024,128,16]{1,0,2:T(8,128)}) fusion(pred[1024]{0:T(1024)(128)(4,1)S(1)} %add_compare_fusion.3, bf16[128,1,16,128]{3,0,2,1:T(8,128)(2,1)S(1)} %get-tuple-element.349, bf16[8,1024,2,1,128]{4,1,3,2,0:T(8,128)(2,1)} %get-tuple-element.346, s32[]{:T(128)S(6)} %select_n.118), kind=kOutput, calls=%fused_computation.1.clone.1 | convolution fusion | flops 543160320 | bytes 9184260 | tf_op jit(solution)/shard_map/while/body/eval_jaxpr/igqd,pgd->igqp/dot_general | solution.py:65
  249.0 5.8 %fusion.85 = f32[128,128,16]{1,0,2:T(8,128)S(1)} fusion(f32[1024,128,16]{1,0,2:T(8,128)} %get-tuple-element.304, f32[128,16]{0,1:T(8,128)S(1)} %max.47, pred[1024]{0:T(1024)(128)(4,1)S(1)} %add_compare_fusion.3, bf16[8,1024,2,1,128]{4,1,3,2,0:T(8,128)(2,1)} %get-tuple-element.346, s32[]{:T(128)S(6)} %select_n.118), kind=kOutput, calls=%fused_computation.8.clone.1 | convolution fusion | flops 547356672 | bytes 9709572 | tf_op jit(solution)/shard_map/while/body/eval_jaxpr/igqp,pgd->igqd/dot_general | solution.py:86
  259.0 4.8 %multiply_reduce_fusion = f32[128,16,128]{0,2,1:T(8,128)S(1)} fusion(f32[8,128,16,128]{1,3,2,0:T(8,128)} %get-tuple-element.146, f32[8,128,16]{1,2,0:T(8,128)S(1)} %get-tuple-element.224), kind=kLoop, calls=%fused_computation.46 | loop fusion | flops 3932160 | bytes 9502720 | tf_op jit(solution)/shard_map/reduce_sum | solution.py:110
  265.7 4.7 %all-to-all-start.3 = ((f32[4,32,2080]{2,1,0:T(8,128)}), f32[4,32,2080]{2,1,0:T(8,128)S(1)}, u32[]{:S(2)}, u32[]{:S(2)}) async-start(f32[4,32,2080]{2,1,0:T(8,128)} %concatenate.17), calls=%async_computation.3 | async-start | bytes 2228224 | tf_op jit(solution)/shard_map/all_to_all | solution.py:114
  271.7 13.1 %all-to-all-done.3 = f32[4,32,2080]{2,1,0:T(8,128)S(1)} async-done(((f32[4,32,2080]{2,1,0:T(8,128)}), f32[4,32,2080]{2,1,0:T(8,128)S(1)}, u32[]{:S(2)}, u32[]{:S(2)}) %all-to-all-start.3) | async-done | bytes 1064992 | tf_op jit(solution)/shard_map/all_to_all | solution.py:114
  (151 shorter events, 41.6 us)
Async XLA Ops:
  0.0 44.4 %copy-start = (bf16[32,128]{1,0:T(8,128)(2,1)S(1)}, bf16[32,128]{1,0:T(8,128)(2,1)}, u32[]{:S(2)}) copy-start(bf16[32,128]{1,0:T(8,128)(2,1)} %param.13) | copy-start | bytes 24580
  17.8 16.8 %all-to-all-start.2 = ((bf16[4,32,2048]{2,1,0:T(8,128)(2,1)}), bf16[4,32,2048]{2,1,0:T(8,128)(2,1)S(1)}, u32[]{:S(2)}, u32[]{:S(2)}) async-start(bf16[4,32,2048]{2,1,0:T(8,128)(2,1)} %stack.10), calls=%async_computation.2 | async-start | bytes 1048576 | tf_op jit(solution)/shard_map/all_to_all | solution.py:43
  30.3 10.9 %copy-start.3 = (s32[8]{0:T(128)S(1)}, s32[8]{0:T(128)}, u32[]{:S(2)}) copy-start(s32[8]{0:T(128)} %param.17) | copy-start | bytes 100
  30.3 11.5 %copy-start.2 = (s32[8,128]{1,0:T(8,128)S(1)}, s32[8,128]{1,0:T(8,128)}, u32[]{:S(2)}) copy-start(s32[8,128]{1,0:T(8,128)} %param.15) | copy-start | bytes 12292
  34.6 57.5 %all-to-all-start = ((bf16[8,1024,256]{1,2,0:T(8,128)(2,1)}), bf16[8,1024,256]{1,2,0:T(8,128)(2,1)}, u32[]{:S(2)}, u32[]{:S(2)}) async-start(bf16[8,1024,256]{1,2,0:T(8,128)(2,1)} %pad_maximum_fusion), calls=%async_computation | async-start | bytes 8388608 | tf_op jit(solution)/shard_map/all_to_all | solution.py:47
  41.2 57.3 %copy-start.1 = (bf16[32,128]{1,0:T(8,128)(2,1)S(1)}, bf16[32,128]{1,0:T(8,128)(2,1)}, u32[]{:S(2)}) copy-start(bf16[32,128]{1,0:T(8,128)(2,1)} %param.14) | copy-start | bytes 24580
  108.6 5.9 %slice-start = ((s8[8388608]{0:T(1024)(128)(4,1)}), s8[4194304]{0:T(1024)(128)(4,1)S(1)}, s32[]{:S(2)}) async-start(s8[8388608]{0:T(1024)(128)(4,1)} %bitcast.165), calls=%async_computation.4 | async-start | bytes 8388608 | tf_op jit(solution)/shard_map/while
  108.7 5.9 %slice-start.1 = ((s8[8388608]{0:T(1024)(128)(4,1)}), s8[4194304]{0:T(1024)(128)(4,1)S(1)}, s32[]{:S(2)}) async-start(s8[8388608]{0:T(1024)(128)(4,1)} %bitcast.165), calls=%async_computation.5 | async-start | bytes 8388608 | tf_op jit(solution)/shard_map/while
  128.6 5.9 %slice-start = ((s8[8388608]{0:T(1024)(128)(4,1)}), s8[4194304]{0:T(1024)(128)(4,1)S(1)}, s32[]{:S(2)}) async-start(s8[8388608]{0:T(1024)(128)(4,1)} %bitcast.165), calls=%async_computation.4 | async-start | bytes 8388608 | tf_op jit(solution)/shard_map/while
  128.7 5.9 %slice-start.1 = ((s8[8388608]{0:T(1024)(128)(4,1)}), s8[4194304]{0:T(1024)(128)(4,1)S(1)}, s32[]{:S(2)}) async-start(s8[8388608]{0:T(1024)(128)(4,1)} %bitcast.165), calls=%async_computation.5 | async-start | bytes 8388608 | tf_op jit(solution)/shard_map/while
  148.7 5.9 %slice-start = ((s8[8388608]{0:T(1024)(128)(4,1)}), s8[4194304]{0:T(1024)(128)(4,1)S(1)}, s32[]{:S(2)}) async-start(s8[8388608]{0:T(1024)(128)(4,1)} %bitcast.165), calls=%async_computation.4 | async-start | bytes 8388608 | tf_op jit(solution)/shard_map/while
  148.8 5.9 %slice-start.1 = ((s8[8388608]{0:T(1024)(128)(4,1)}), s8[4194304]{0:T(1024)(128)(4,1)S(1)}, s32[]{:S(2)}) async-start(s8[8388608]{0:T(1024)(128)(4,1)} %bitcast.165), calls=%async_computation.5 | async-start | bytes 8388608 | tf_op jit(solution)/shard_map/while
  168.7 5.9 %slice-start = ((s8[8388608]{0:T(1024)(128)(4,1)}), s8[4194304]{0:T(1024)(128)(4,1)S(1)}, s32[]{:S(2)}) async-start(s8[8388608]{0:T(1024)(128)(4,1)} %bitcast.165), calls=%async_computation.4 | async-start | bytes 8388608 | tf_op jit(solution)/shard_map/while
  168.8 5.9 %slice-start.1 = ((s8[8388608]{0:T(1024)(128)(4,1)}), s8[4194304]{0:T(1024)(128)(4,1)S(1)}, s32[]{:S(2)}) async-start(s8[8388608]{0:T(1024)(128)(4,1)} %bitcast.165), calls=%async_computation.5 | async-start | bytes 8388608 | tf_op jit(solution)/shard_map/while
  188.8 5.9 %slice-start = ((s8[8388608]{0:T(1024)(128)(4,1)}), s8[4194304]{0:T(1024)(128)(4,1)S(1)}, s32[]{:S(2)}) async-start(s8[8388608]{0:T(1024)(128)(4,1)} %bitcast.165), calls=%async_computation.4 | async-start | bytes 8388608 | tf_op jit(solution)/shard_map/while
  188.9 5.9 %slice-start.1 = ((s8[8388608]{0:T(1024)(128)(4,1)}), s8[4194304]{0:T(1024)(128)(4,1)S(1)}, s32[]{:S(2)}) async-start(s8[8388608]{0:T(1024)(128)(4,1)} %bitcast.165), calls=%async_computation.5 | async-start | bytes 8388608 | tf_op jit(solution)/shard_map/while
  208.8 5.9 %slice-start = ((s8[8388608]{0:T(1024)(128)(4,1)}), s8[4194304]{0:T(1024)(128)(4,1)S(1)}, s32[]{:S(2)}) async-start(s8[8388608]{0:T(1024)(128)(4,1)} %bitcast.165), calls=%async_computation.4 | async-start | bytes 8388608 | tf_op jit(solution)/shard_map/while
  208.9 5.9 %slice-start.1 = ((s8[8388608]{0:T(1024)(128)(4,1)}), s8[4194304]{0:T(1024)(128)(4,1)S(1)}, s32[]{:S(2)}) async-start(s8[8388608]{0:T(1024)(128)(4,1)} %bitcast.165), calls=%async_computation.5 | async-start | bytes 8388608 | tf_op jit(solution)/shard_map/while
  228.9 5.9 %slice-start = ((s8[8388608]{0:T(1024)(128)(4,1)}), s8[4194304]{0:T(1024)(128)(4,1)S(1)}, s32[]{:S(2)}) async-start(s8[8388608]{0:T(1024)(128)(4,1)} %bitcast.165), calls=%async_computation.4 | async-start | bytes 8388608 | tf_op jit(solution)/shard_map/while
  229.0 5.9 %slice-start.1 = ((s8[8388608]{0:T(1024)(128)(4,1)}), s8[4194304]{0:T(1024)(128)(4,1)S(1)}, s32[]{:S(2)}) async-start(s8[8388608]{0:T(1024)(128)(4,1)} %bitcast.165), calls=%async_computation.5 | async-start | bytes 8388608 | tf_op jit(solution)/shard_map/while
  248.9 5.9 %slice-start = ((s8[8388608]{0:T(1024)(128)(4,1)}), s8[4194304]{0:T(1024)(128)(4,1)S(1)}, s32[]{:S(2)}) async-start(s8[8388608]{0:T(1024)(128)(4,1)} %bitcast.165), calls=%async_computation.4 | async-start | bytes 8388608 | tf_op jit(solution)/shard_map/while
  249.0 5.9 %slice-start.1 = ((s8[8388608]{0:T(1024)(128)(4,1)}), s8[4194304]{0:T(1024)(128)(4,1)S(1)}, s32[]{:S(2)}) async-start(s8[8388608]{0:T(1024)(128)(4,1)} %bitcast.165), calls=%async_computation.5 | async-start | bytes 8388608 | tf_op jit(solution)/shard_map/while
  259.0 11.4 %copy-start.4 = (s32[8]{0:T(128)S(1)}, s32[8]{0:T(128)}, u32[]{:S(2)}) copy-start(s32[8]{0:T(128)} %param.16) | copy-start | bytes 100
  265.7 19.0 %all-to-all-start.3 = ((f32[4,32,2080]{2,1,0:T(8,128)}), f32[4,32,2080]{2,1,0:T(8,128)S(1)}, u32[]{:S(2)}, u32[]{:S(2)}) async-start(f32[4,32,2080]{2,1,0:T(8,128)} %concatenate.17), calls=%async_computation.3 | async-start | bytes 2228224 | tf_op jit(solution)/shard_map/all_to_all | solution.py:114
